TPU v7x, 256 devices: a whole 4x4x8 slice. The times are simulated.
256 devices in a mesh: gx: 32 (over x_hi, z, core), gy: 8 (over x_lo, y).
Axes of the slice: x: 4 (x_hi: 2, x_lo: 2; x = x_hi * 2 + x_lo), y: 4, z: 8, core: 2. Of those that a mesh axis runs over, the one named last changes fastest.
Arguments:
- background: bfloat16 [2, 2048, 1024, 128], P(None, 'gx', 'gy'), may hold values from -6 to 6
- observation_cell_index: int32 [32, 8, 512], P('gx', 'gy'), may hold values from 0 to 16383
- obs_value: float32 [32, 8, 512], P('gx', 'gy'), may hold values from -6 to 6
- obs_inverse: float32 [32, 8, 512], P('gx', 'gy'), may hold values from 0.5 to 4
- obs_count: int32 [32, 8], P('gx', 'gy'), may hold values from 256 to 512, as said below
- taper: int32 [64], replicated, may hold values from 32 to 1024
Outputs:
- analysis: bfloat16 [2, 2048, 1024, 128], P(None, 'gx', 'gy')
Inputs may be any that keep to these rules, and one draw needn't show every extreme that they name: `obs_count`: some tile has exactly 512 live slots and some tile exactly 256.
All inputs are finite; a program needn't handle non-finite values.
Results may differ from a plain program's by a relative error of at most 0.0028.
The roundings to bfloat16 on the way count: a program that leaves them out, or rounds other values in their place, can miss the bound.
Values may be sent and summed in bfloat16 or wider, within the bound.
A program may use at most 64 MiB of HBM per device.

v0:
```python
import jax
import jax.numpy as jnp
from jax import lax
from jax.sharding import PartitionSpec as P

NSTEPS = 6
HIGH = lax.Precision.HIGHEST


def extended(cells, sides, width):
    for axis, dim in sides:
        count = lax.axis_size(axis)
        ends = count - 1
        head = lax.slice_in_dim(cells, 0, width, axis=dim)
        tail = lax.slice_in_dim(cells, cells.shape[dim] - width, cells.shape[dim], axis=dim)
        cells = jnp.concatenate(
            [
                lax.ppermute(tail, axis, [(i, (i + 1) % count) for i in range(ends)]),
                cells,
                lax.ppermute(head, axis, [((i + 1) % count, i) for i in range(ends)]),
            ],
            axis=dim,
        )
    return cells


def observe(ensemble, cell_ids, values, inverse, live_count, tile_x, tile_y):
    picked = jnp.take(ensemble, cell_ids, axis=0).astype(jnp.float32)
    center = jnp.mean(picked, axis=1)
    perturb = (picked - center[:, None]).astype(jnp.bfloat16)
    slot_ids = jnp.arange(cell_ids.shape[0], dtype=jnp.int32)
    live_mask = (slot_ids < live_count).astype(jnp.float32)
    column_pos = cell_ids % (tile_x * tile_y) // tile_y
    row_pos = cell_ids % tile_y
    metadata = jnp.stack(
        [
            values - center,
            inverse * live_mask,
            column_pos.astype(jnp.float32),
            row_pos.astype(jnp.float32),
        ]
    ).astype(jnp.bfloat16)
    return (perturb, metadata, live_mask)


def statistics(perturb, metadata, live_mask):
    members = perturb.shape[1]
    weight = metadata[1].astype(jnp.float32)
    innovation = metadata[0].astype(jnp.float32)
    spread = jnp.sum(jnp.square(perturb.astype(jnp.float32)), axis=1) / (members - 1)
    return (
        jnp.sum(weight * innovation * innovation),
        jnp.sum(weight * spread) + jnp.sum(live_mask),
    )


def transform(perturb9, metadata9, inflation, taper, tile_x, tile_y):
    members = perturb9.shape[-1]
    bins = taper.shape[0]
    offsets = jnp.arange(3, dtype=jnp.int32) - 1
    column_pos = offsets[:, None, None] * tile_x + metadata9[:, :, 2, :].astype(jnp.int32)
    row_pos = offsets[None, :, None] * tile_y + metadata9[:, :, 3, :].astype(jnp.int32)
    delta_x = 2 * column_pos - (tile_x - 1)
    delta_y = 2 * row_pos - (tile_y - 1)
    distance = (delta_x * delta_x + delta_y * delta_y) * bins
    limit = 9 * (tile_x * tile_x + tile_y * tile_y)
    bin_edges = jnp.arange(bins, dtype=jnp.int32) * limit
    in_bin = (distance[..., None] >= bin_edges) & (distance[..., None] < bin_edges + limit)
    tapered_weight_factor = (
        jnp.sum(jnp.where(in_bin, taper.astype(jnp.float32), jnp.float32(0.0)), axis=-1) / 1024.0
    )
    effective = metadata9[:, :, 1, :].astype(jnp.float32) * tapered_weight_factor
    flat = perturb9.reshape(-1, members)
    weighted = (flat.astype(jnp.float32) * effective.reshape(-1)[:, None]).astype(jnp.bfloat16)
    gram_matrix = lax.dot_general(
        weighted, flat, (((0,), (0,)), ((), ())), preferred_element_type=jnp.float32
    )
    innovation = metadata9[:, :, 0, :].reshape(1, -1)
    projected = jnp.dot(innovation, weighted, preferred_element_type=jnp.float32)[0]
    identity = jnp.eye(members, dtype=jnp.float32)
    system = identity / inflation + gram_matrix / (members - 1)
    frobenius = jnp.sqrt(jnp.sum(system * system))
    root_iter = system / frobenius
    inverse_root = identity
    for sweep in range(NSTEPS):
        correction = 1.5 * identity - 0.5 * jnp.dot(
            inverse_root, root_iter, precision=HIGH, preferred_element_type=jnp.float32
        )
        root_iter = jnp.dot(
            root_iter, correction, precision=HIGH, preferred_element_type=jnp.float32
        )
        inverse_root = jnp.dot(
            correction, inverse_root, precision=HIGH, preferred_element_type=jnp.float32
        )
    spread_weights = inverse_root / jnp.sqrt(frobenius)
    inner = jnp.dot(inverse_root, projected, precision=HIGH, preferred_element_type=jnp.float32)
    mean_weights = jnp.dot(
        inverse_root, inner, precision=HIGH, preferred_element_type=jnp.float32
    ) / (frobenius * (members - 1))
    return (spread_weights + mean_weights[:, None]).astype(jnp.bfloat16)


def spline(length, tile_id, tiles):
    position = (jnp.arange(length, dtype=jnp.float32) + 0.5) / length
    left_part = 0.5 * jnp.square(1.0 - position)
    middle = 0.5 + position - jnp.square(position)
    right_part = 0.5 * jnp.square(position)
    has_left = (tile_id > 0).astype(jnp.float32)
    has_right = (tile_id < tiles - 1).astype(jnp.float32)
    middle = middle + (1.0 - has_left) * left_part + (1.0 - has_right) * right_part
    return jnp.stack([left_part * has_left, middle, right_part * has_right])


def blend(ensemble, weights9, column_id, row_id, columns, row_tiles):
    levels, tile_x, tile_y, members = ensemble.shape
    widened = ensemble.astype(jnp.float32)
    center = jnp.mean(widened, axis=-1, keepdims=True)
    deviation = widened - center
    beta_x = spline(tile_x, column_id, columns)
    beta_y = spline(tile_y, row_id, row_tiles)
    analysis = center
    for offset_y in range(3):
        pieces = [
            (
                deviation
                * (beta_x[offset_x][:, None] * beta_y[offset_y][None, :])[None, :, :, None]
            ).astype(jnp.bfloat16)
            for offset_x in range(3)
        ]
        stacked = jnp.concatenate(pieces, axis=-1).reshape(-1, 3 * members)
        column_stack = weights9[:, offset_y].reshape(3 * members, members)
        product = jnp.dot(stacked, column_stack, preferred_element_type=jnp.float32)
        analysis = analysis + product.reshape(levels, tile_x, tile_y, members)
    return analysis.astype(jnp.bfloat16)


def local(background, observation_cell_index, obs_value, obs_inverse, obs_count, taper):
    levels, tile_x, tile_y, members = background.shape
    slot_total = observation_cell_index.shape[2]
    ensemble = background.reshape(-1, members)
    perturb, metadata, live_mask = observe(
        ensemble,
        observation_cell_index[0, 0],
        obs_value[0, 0],
        obs_inverse[0, 0],
        obs_count[0, 0],
        tile_x,
        tile_y,
    )
    numerator, denominator = statistics(perturb, metadata, live_mask)
    numerator, denominator = lax.psum((numerator, denominator), ("gx", "gy"))
    inflation = numerator / denominator
    packed = jnp.concatenate([perturb, metadata.reshape(-1, members)], axis=0)[None, None]
    adjacent_tiles = extended(packed, (("gx", 0), ("gy", 1)), 1)
    neighbour_perturbation_rows = adjacent_tiles[:, :, :slot_total]
    neighbour_metadata_rows = adjacent_tiles[:, :, slot_total:].reshape(3, 3, 4, slot_total)
    tile_weights = transform(
        neighbour_perturbation_rows, neighbour_metadata_rows, inflation, taper, tile_x, tile_y
    )[None, None]
    near_weights = extended(tile_weights, (("gx", 0), ("gy", 1)), 1)
    return blend(
        background,
        near_weights,
        lax.axis_index("gx"),
        lax.axis_index("gy"),
        lax.axis_size("gx"),
        lax.axis_size("gy"),
    )


def solution(mesh):
    in_specs = (
        P(None, "gx", "gy", None),
        P("gx", "gy", None),
        P("gx", "gy", None),
        P("gx", "gy", None),
        P("gx", "gy"),
        P(),
    )
    out_specs = P(None, "gx", "gy", None)
    return jax.shard_map(local, mesh=mesh, in_specs=in_specs, out_specs=out_specs, check_vma=False)
```

profile of v0, /device:TPU:2, one launch (start us, length us, event | category | flops | bytes accessed | tf_op | source)
XLA Modules:
  0.0 185.3 jit_solution(1450910014959891026)
XLA Ops:
  0.0 0.0 copy-start
  0.0 0.7 fusion.60
  0.7 0.7 compare_select_fusion
  2.1 0.7 compare_and_fusion
  2.8 3.8 %gather_fusion = bf16[512,128]{1,0:T(8,128)(2,1)S(1)} fusion(bf16[16384,128]{1,0:T(8,128)(2,1)} %bitcast.130, s32[1024]{0:T(1024)S(1)} %pad_clamp_fusion), kind=kCustom, calls=%fused_computation | custom fusion | bytes 264192 | tf_op jit(solution)/shard_map/jit(_take)/gather | solution.py:28
  6.6 0.2 convert_reduce_fusion.1
  6.8 0.3 multiply_reduce_fusion
  7.1 0.7 compare_select_fusion.1
  7.9 1.3 collective-permute-start.1
  9.2 3.0 %collective-permute-start = (bf16[1,1,528,128]{3,2,1,0:T(8,128)(2,1)S(1)}, bf16[1,1,528,128]{3,2,1,0:T(8,128)(2,1)S(1)}, u32[]{:S(2)}, u32[]{:S(2)}) collective-permute-start(bf16[1,1,528,128]{3,2,1,0:T(8,128)(2,1)S(1)} %maximum_bitcast_fusion), channel_id=1, source_target_pairs={{0,8},{8,16},{16,24},{24,32},{32,40},{40,48},{48,56},{56,64},{64,7... | collective-permute-start | bytes 405512 | tf_op jit(solution)/shard_map/ppermute | solution.py:18
  12.3 3.4 %convert_reduce_fusion = f32[2,64,128]{2,1,0:T(8,128)S(1)} fusion(bf16[2,64,128,128]{3,2,1,0:T(8,128)(2,1)} %param.6), kind=kLoop, calls=%fused_computation.20 | loop fusion | flops 4177920 | bytes 4259840 | tf_op jit(solution)/shard_map/reduce_sum | solution.py:117
  15.7 0.7 fusion.58
  16.4 0.6 convert_reduce_fusion.2
  18.2 83.2 %all-reduce = (f32[]{:T(128)}, f32[]{:T(128)}) all-reduce(f32[]{:T(128)S(6)} %add.238, f32[]{:T(128)} %get-tuple-element.5), channel_id=1, replica_groups=mesh['gx'=32,'gy'=8] {'gx','gy'}, use_global_device_ids=true, to_apply=%region_5.6 | all-reduce | flops 2 | bytes 16 | tf_op jit(solution)/shard_map/psum | solution.py:151
  101.4 0.0 copy-done
  102.7 0.0 collective-permute-done.1
  102.7 0.0 collective-permute-done
  102.8 4.6 %collective-permute-start.3 = (bf16[3,1,528,128]{3,2,1,0:T(8,128)(2,1)S(1)}, bf16[3,1,528,128]{3,2,1,0:T(8,128)(2,1)S(1)}, u32[]{:S(2)}, u32[]{:S(2)}) collective-permute-start(bf16[3,1,528,128]{3,2,1,0:T(8,128)(2,1)S(1)} %pad_maximum_fusion.1), channel_id=1, source_target_pairs={{1,0},{2,1},{3,2},{4,3},{5,4},{6,5},{7,6},{9,8},{10,9},{11,10},{12... | collective-permute-start | bytes 1216520 | tf_op jit(solution)/shard_map/ppermute | solution.py:20
  107.4 1.9 %collective-permute-start.2 = (bf16[3,1,528,128]{3,2,1,0:T(8,128)(2,1)S(1)}, bf16[3,1,528,128]{3,2,1,0:T(8,128)(2,1)S(1)}, u32[]{:S(2)}, u32[]{:S(2)}) collective-permute-start(bf16[3,1,528,128]{3,2,1,0:T(8,128)(2,1)S(1)} %pad_maximum_fusion.1), channel_id=1, source_target_pairs={{0,1},{1,2},{2,3},{3,4},{4,5},{5,6},{6,7},{8,9},{9,10},{10,11},{11... | collective-permute-start | bytes 1216520 | tf_op jit(solution)/shard_map/ppermute | solution.py:18
  109.3 0.1 broadcast_multiply_fusion.3
  109.4 6.6 %collective-permute-done.3 = bf16[3,1,528,128]{3,2,1,0:T(8,128)(2,1)S(1)} collective-permute-done((bf16[3,1,528,128]{3,2,1,0:T(8,128)(2,1)S(1)}, bf16[3,1,528,128]{3,2,1,0:T(8,128)(2,1)S(1)}, u32[]{:S(2)}, u32[]{:S(2)}) %collective-permute-start.3) | collective-permute-done | bytes 405536 | tf_op jit(solution)/shard_map/ppermute | solution.py:20
  116.0 6.2 %collective-permute-done.2 = bf16[3,1,528,128]{3,2,1,0:T(8,128)(2,1)S(1)} collective-permute-done((bf16[3,1,528,128]{3,2,1,0:T(8,128)(2,1)S(1)}, bf16[3,1,528,128]{3,2,1,0:T(8,128)(2,1)S(1)}, u32[]{:S(2)}, u32[]{:S(2)}) %collective-permute-start.2) | collective-permute-done | bytes 405536 | tf_op jit(solution)/shard_map/ppermute | solution.py:18
  122.2 0.1 fusion.71
  122.3 0.1 fusion.54
  122.4 0.3 select_reduce_fusion
  122.7 0.1 pad_maximum_fusion
  122.9 0.8 multiply_convert_fusion
  123.7 1.1 multiply_reduce_fusion.1
  125.5 0.2 fusion.41
  125.7 0.2 fusion.47
  125.9 0.2 fusion.49
  126.1 0.2 fusion.40
  126.3 0.2 fusion.72
  126.5 0.2 fusion.73
  126.7 0.2 fusion.39
  127.0 0.2 fusion.74
  127.2 0.2 fusion.75
  127.4 0.2 fusion.38
  127.6 0.2 fusion.76
  127.8 0.2 fusion.77
  128.0 0.2 fusion.37
  128.2 0.2 fusion.78
  128.4 0.2 fusion.79
  128.7 0.2 fusion.36
  128.9 0.2 fusion.80
  129.1 0.3 convolution_bitcast_fusion.3
  129.4 0.2 convolution_bitcast_fusion.2
  129.6 0.2 fusion.44
  129.8 0.1 fusion.48
  129.9 1.3 collective-permute-start.5
  131.2 3.0 %collective-permute-start.4 = (bf16[1,1,128,128]{3,2,1,0:T(8,128)(2,1)S(1)}, bf16[1,1,128,128]{3,2,1,0:T(8,128)(2,1)S(1)}, u32[]{:S(2)}, u32[]{:S(2)}) collective-permute-start(bf16[1,1,128,128]{3,2,1,0:T(8,128)(2,1)S(1)} %fusion.48), channel_id=1, source_target_pairs={{0,8},{8,16},{16,24},{24,32},{32,40},{40,48},{48,56},{56,64},{64,7... | collective-permute-start | bytes 98312 | tf_op jit(solution)/shard_map/ppermute | solution.py:18
  134.3 17.4 %fusion.33 = (bf16[2,64,128,128]{3,2,1,0:T(8,128)(2,1)S(1)}, bf16[2,64,128,128]{3,2,1,0:T(8,128)(2,1)S(1)}, bf16[2,64,128,128]{3,2,1,0:T(8,128)(2,1)S(1)}, bf16[...) fusion(bf16[2,64,128,128]{3,2,1,0:T(8,128)(2,1)} %param.6, ...), kind=kLoop, calls=%fused_computation.36 | loop fusion | flops 41943040 | bytes 42303488 | tf_op jit(solution)/shard_map/convert_element_type | solution.py:127
  151.6 0.0 collective-permute-done.5
  151.6 0.0 collective-permute-done.4
  151.7 1.9 %collective-permute-start.6 = (bf16[3,1,128,128]{3,2,1,0:T(8,128)(2,1)S(1)}, bf16[3,1,128,128]{3,2,1,0:T(8,128)(2,1)S(1)}, u32[]{:S(2)}, u32[]{:S(2)}) collective-permute-start(bf16[3,1,128,128]{3,2,1,0:T(8,128)(2,1)S(1)} %pad_maximum_fusion.2), channel_id=1, source_target_pairs={{0,1},{1,2},{2,3},{3,4},{4,5},{5,6},{6,7},{8,9},{9,10},{10,11},{11... | collective-permute-start | bytes 294920 | tf_op jit(solution)/shard_map/ppermute | solution.py:18
  153.6 6.0 %collective-permute-start.7 = (bf16[3,1,128,128]{3,2,1,0:T(8,128)(2,1)S(1)}, bf16[3,1,128,128]{3,2,1,0:T(8,128)(2,1)S(1)}, u32[]{:S(2)}, u32[]{:S(2)}) collective-permute-start(bf16[3,1,128,128]{3,2,1,0:T(8,128)(2,1)S(1)} %pad_maximum_fusion.2), channel_id=1, source_target_pairs={{1,0},{2,1},{3,2},{4,3},{5,4},{6,5},{7,6},{9,8},{10,9},{11,10},{12... | collective-permute-start | bytes 294920 | tf_op jit(solution)/shard_map/ppermute | solution.py:20
  159.6 8.5 %fusion.6 = f32[2,64,128,128]{3,2,1,0:T(8,128)} fusion(bf16[384,128,1,1]{1,0,3,2:T(8,128)(2,1)S(1)} %bitcast.132, bf16[2,64,128,128]{3,2,1,0:T(8,128)(2,1)} %get-tuple-element.16, bf16[2,64,128,128]{3,2,1,0:T(8,128)(2,1)} %get-tuple-element.15, bf16[2,64,128,128]{3,2,1,0:T(8,128)(2,1)} %get-tuple-element.14), kind=kOutput, calls=%fused_computation.7 | convolution fusion | flops 1648361472 | bytes 21069824 | tf_op jit(solution)/shard_map/dot_general | solution.py:132
  168.1 0.0 collective-permute-done.6
  168.1 5.7 %fusion = f32[2,64,128,128]{3,2,1,0:T(8,128)} fusion(bf16[384,128,1,1]{1,0,3,2:T(8,128)(2,1)S(1)} %bitcast.140, bf16[2,64,128,128]{3,2,1,0:T(8,128)(2,1)S(1)} %get-tuple-element.13, bf16[2,64,128,128]{3,2,1,0:T(8,128)(2,1)S(1)} %get-tuple-element.12, bf16[2,64,128,128]{3,2,1,0:T(8,128)(2,1)S(1)} %get-tuple-element.19), kind=kOutput, calls=%fused_computation.1 | convolution fusion | flops 1648361472 | bytes 21069824 | tf_op jit(solution)/shard_map/dot_general | solution.py:132
  173.8 0.0 collective-permute-done.7
  173.8 11.4 %add_convert_fusion = bf16[2,64,128,128]{3,2,1,0:T(8,128)(2,1)} fusion(f32[2,64,128,128]{3,2,1,0:T(8,128)} %fusion.6, f32[2,64,128,128]{3,2,1,0:T(8,128)} %fusion, f32[2,64,128]{2,1,0:T(8,128)S(1)} %broadcast_multiply_fusion, bf16[384,128,1,1]{1,0,3,2:T(8,128)(2,1)S(1)} %bitcast.139, bf16[2,64,128,128]{3,2,1,0:T(8,128)(2,1)S(1)} %get-tuple-element.18, ...), kind=kOutput, calls=%fused_computation.39 | convolution fusion | flops 1656750080 | bytes 33718272 | tf_op jit(solution)/shard_map/dot_general | solution.py:132
  (19 shorter events, 0.2 us)
Async XLA Ops:
  0.0 101.4 %copy-start = (s32[64]{0:T(128)S(1)}, s32[64]{0:T(128)}, u32[]{:S(2)}) copy-start(s32[64]{0:T(128)} %param.11) | copy-start | bytes 772
  7.9 94.9 %collective-permute-start.1 = (bf16[1,1,528,128]{3,2,1,0:T(8,128)(2,1)S(1)}, bf16[1,1,528,128]{3,2,1,0:T(8,128)(2,1)S(1)}, u32[]{:S(2)}, u32[]{:S(2)}) collective-permute-start(bf16[1,1,528,128]{3,2,1,0:T(8,128)(2,1)S(1)} %maximum_bitcast_fusion), channel_id=1, source_target_pairs={{8,0},{16,8},{24,16},{32,24},{40,32},{48,40},{56,48},{64,56},{72,6... | collective-permute-start | bytes 405512 | tf_op jit(solution)/shard_map/ppermute | solution.py:20
  9.2 93.6 %collective-permute-start = (bf16[1,1,528,128]{3,2,1,0:T(8,128)(2,1)S(1)}, bf16[1,1,528,128]{3,2,1,0:T(8,128)(2,1)S(1)}, u32[]{:S(2)}, u32[]{:S(2)}) collective-permute-start(bf16[1,1,528,128]{3,2,1,0:T(8,128)(2,1)S(1)} %maximum_bitcast_fusion), channel_id=1, source_target_pairs={{0,8},{8,16},{16,24},{24,32},{32,40},{40,48},{48,56},{56,64},{64,7... | collective-permute-start | bytes 405512 | tf_op jit(solution)/shard_map/ppermute | solution.py:18
  102.8 13.2 %collective-permute-start.3 = (bf16[3,1,528,128]{3,2,1,0:T(8,128)(2,1)S(1)}, bf16[3,1,528,128]{3,2,1,0:T(8,128)(2,1)S(1)}, u32[]{:S(2)}, u32[]{:S(2)}) collective-permute-start(bf16[3,1,528,128]{3,2,1,0:T(8,128)(2,1)S(1)} %pad_maximum_fusion.1), channel_id=1, source_target_pairs={{1,0},{2,1},{3,2},{4,3},{5,4},{6,5},{7,6},{9,8},{10,9},{11,10},{12... | collective-permute-start | bytes 1216520 | tf_op jit(solution)/shard_map/ppermute | solution.py:20
  107.4 14.8 %collective-permute-start.2 = (bf16[3,1,528,128]{3,2,1,0:T(8,128)(2,1)S(1)}, bf16[3,1,528,128]{3,2,1,0:T(8,128)(2,1)S(1)}, u32[]{:S(2)}, u32[]{:S(2)}) collective-permute-start(bf16[3,1,528,128]{3,2,1,0:T(8,128)(2,1)S(1)} %pad_maximum_fusion.1), channel_id=1, source_target_pairs={{0,1},{1,2},{2,3},{3,4},{4,5},{5,6},{6,7},{8,9},{9,10},{10,11},{11... | collective-permute-start | bytes 1216520 | tf_op jit(solution)/shard_map/ppermute | solution.py:18
  129.9 21.7 %collective-permute-start.5 = (bf16[1,1,128,128]{3,2,1,0:T(8,128)(2,1)S(1)}, bf16[1,1,128,128]{3,2,1,0:T(8,128)(2,1)S(1)}, u32[]{:S(2)}, u32[]{:S(2)}) collective-permute-start(bf16[1,1,128,128]{3,2,1,0:T(8,128)(2,1)S(1)} %fusion.48), channel_id=1, source_target_pairs={{8,0},{16,8},{24,16},{32,24},{40,32},{48,40},{56,48},{64,56},{72,6... | collective-permute-start | bytes 98312 | tf_op jit(solution)/shard_map/ppermute | solution.py:20
  131.2 20.4 %collective-permute-start.4 = (bf16[1,1,128,128]{3,2,1,0:T(8,128)(2,1)S(1)}, bf16[1,1,128,128]{3,2,1,0:T(8,128)(2,1)S(1)}, u32[]{:S(2)}, u32[]{:S(2)}) collective-permute-start(bf16[1,1,128,128]{3,2,1,0:T(8,128)(2,1)S(1)} %fusion.48), channel_id=1, source_target_pairs={{0,8},{8,16},{16,24},{24,32},{32,40},{40,48},{48,56},{56,64},{64,7... | collective-permute-start | bytes 98312 | tf_op jit(solution)/shard_map/ppermute | solution.py:18
  151.7 16.5 %collective-permute-start.6 = (bf16[3,1,128,128]{3,2,1,0:T(8,128)(2,1)S(1)}, bf16[3,1,128,128]{3,2,1,0:T(8,128)(2,1)S(1)}, u32[]{:S(2)}, u32[]{:S(2)}) collective-permute-start(bf16[3,1,128,128]{3,2,1,0:T(8,128)(2,1)S(1)} %pad_maximum_fusion.2), channel_id=1, source_target_pairs={{0,1},{1,2},{2,3},{3,4},{4,5},{5,6},{6,7},{8,9},{9,10},{10,11},{11... | collective-permute-start | bytes 294920 | tf_op jit(solution)/shard_map/ppermute | solution.py:18
  153.6 20.2 %collective-permute-start.7 = (bf16[3,1,128,128]{3,2,1,0:T(8,128)(2,1)S(1)}, bf16[3,1,128,128]{3,2,1,0:T(8,128)(2,1)S(1)}, u32[]{:S(2)}, u32[]{:S(2)}) collective-permute-start(bf16[3,1,128,128]{3,2,1,0:T(8,128)(2,1)S(1)} %pad_maximum_fusion.2), channel_id=1, source_target_pairs={{1,0},{2,1},{3,2},{4,3},{5,4},{6,5},{7,6},{9,8},{10,9},{11,10},{12... | collective-permute-start | bytes 294920 | tf_op jit(solution)/shard_map/ppermute | solution.py:20
where the time goes:
time: 186 us; the launch traced here: 185 us
  blocking collectives  83.2 us (45%)
  matrix products  30.8 us (17%)
  other arithmetic  27.2 us (15%)
  starting transfers between devices  23.1 us (12%)
  waiting for transfers between devices  12.8 us (7%)
  between operations  4.26 us (2%)
  local copies, waits for them, and re-layouts  3.82 us (2%)
    psum x1, blocking collectives, local(): numerator, denominator = lax.psum((numerator, denominator), ('gx', 'gy'))  83.2 us
    dot_general x3, matrix products, blend(): product = jnp.dot(stacked, column_stack, preferred_element_type=jnp.float32)  25.6 us
    convert_element_type x1, other arithmetic, blend(): pieces = [(deviation * (beta_x[offset_x][:, None] * beta_y[offset_y][None...  17.4 us
    ppermute x4, starting transfers between devices, extended(): lax.ppermute(head, axis, [((i + 1) % count, i) for i in range(ends)])  13.2 us
    ppermute x4, starting transfers between devices, extended(): lax.ppermute(tail, axis, [(i, (i + 1) % count) for i in range(ends)])  9.91 us
    ppermute x4, waiting for transfers between devices, extended(): lax.ppermute(head, axis, [((i + 1) % count, i) for i in range(ends)])  6.56 us
    ppermute x4, waiting for transfers between devices, extended(): lax.ppermute(tail, axis, [(i, (i + 1) % count) for i in range(ends)])  6.23 us
    gather x1, local copies, waits for them, and re-layouts, observe(): picked = jnp.take(ensemble, cell_ids, axis=0).astype(jnp.float32)  3.78 us
  transfers between devices with their start and end apart: 8, of which 2 were waited for; matrix products, arithmetic and copies ran while one was open for 20% of the time, Pallas kernels for 0%

commit v1 on v0

--- a/solution.py
+++ b/solution.py
@@ -148,7 +148,7 @@
         tile_y,
     )
     numerator, denominator = statistics(perturb, metadata, live_mask)
-    numerator, denominator = lax.psum((numerator, denominator), ("gx", "gy"))
+    numerator, denominator = lax.psum(lax.psum((numerator, denominator), "gy"), "gx")
     inflation = numerator / denominator
     packed = jnp.concatenate([perturb, metadata.reshape(-1, members)], axis=0)[None, None]
     adjacent_tiles = extended(packed, (("gx", 0), ("gy", 1)), 1)

time: 186 us -> 191 us (1.027); the launches traced: 185 us -> 188 us
  blocking collectives: 83.2 us -> 88.1 us
  waiting for transfers between devices: 12.8 us -> 10.7 us
    psum x1 -> x2, blocking collectives: 83.2 us -> 88.1 us  [the longest x1 68.3 us: local(): lax.psum(lax.psum((numerator, denominator), 'gy'), 'gx')]
    ppermute x4, waiting for transfers between devices: 6.23 us -> 4.11 us  [extended(): lax.ppermute(tail, axis, [(i, (i + 1) % count) for i in range(ends)])]
    ppermute x4, starting transfers between devices: 13.2 us -> 11.2 us  [extended(): lax.ppermute(head, axis, [((i + 1) % count, i) for i in range(ends)])]
  transfers between devices with their start and end apart: 8 -> 8, of which waited for: 2 -> 2; matrix products, arithmetic and copies ran while one was open for 20% -> 19% of each run, Pallas kernels for 0% -> 0%
where the time goes in v1:
time: 191 us; the launch traced here: 188 us
  blocking collectives  88.1 us (46%)
  matrix products  30.8 us (16%)
  other arithmetic  27.2 us (14%)
  starting transfers between devices  22.4 us (12%)
  waiting for transfers between devices  10.7 us (6%)
  between operations  4.39 us (2%)
  local copies, waits for them, and re-layouts  3.82 us (2%)
    psum x1, blocking collectives, local(): lax.psum(lax.psum((numerator, denominator), 'gy'), 'gx')  68.3 us
    dot_general x3, matrix products, blend(): product = jnp.dot(stacked, column_stack, preferred_element_type=jnp.float32)  25.6 us
    psum x1, blocking collectives, local(): lax.psum((numerator, denominator), 'gy')  19.8 us
    convert_element_type x1, other arithmetic, blend(): pieces = [(deviation * (beta_x[offset_x][:, None] * beta_y[offset_y][None...  17.4 us
    ppermute x4, starting transfers between devices, extended(): lax.ppermute(tail, axis, [(i, (i + 1) % count) for i in range(ends)])  11.3 us
    ppermute x4, starting transfers between devices, extended(): lax.ppermute(head, axis, [((i + 1) % count, i) for i in range(ends)])  11.2 us
    ppermute x4, waiting for transfers between devices, extended(): lax.ppermute(head, axis, [((i + 1) % count, i) for i in range(ends)])  6.64 us
    ppermute x4, waiting for transfers between devices, extended(): lax.ppermute(tail, axis, [(i, (i + 1) % count) for i in range(ends)])  4.11 us
  transfers between devices with their start and end apart: 8, of which 2 were waited for; matrix products, arithmetic and copies ran while one was open for 19% of the time, Pallas kernels for 0%

profile of v1, /device:TPU:2, one launch (start us, length us, event | category | flops | bytes accessed | tf_op | source)
XLA Modules:
  0.0 187.5 jit_solution(1732813800015669945)
XLA Ops:
  0.0 0.0 copy-start
  0.0 0.7 fusion.60
  0.7 0.7 compare_select_fusion
  2.1 0.7 compare_and_fusion
  2.8 3.8 %gather_fusion = bf16[512,128]{1,0:T(8,128)(2,1)S(1)} fusion(bf16[16384,128]{1,0:T(8,128)(2,1)} %bitcast.130, s32[1024]{0:T(1024)S(1)} %pad_clamp_fusion), kind=kCustom, calls=%fused_computation | custom fusion | bytes 264192 | tf_op jit(solution)/shard_map/jit(_take)/gather | solution.py:28
  6.6 0.2 convert_reduce_fusion.1
  6.8 0.3 multiply_reduce_fusion
  7.1 0.7 compare_select_fusion.1
  7.9 1.3 collective-permute-start.1
  9.2 3.0 %collective-permute-start = (bf16[1,1,528,128]{3,2,1,0:T(8,128)(2,1)S(1)}, bf16[1,1,528,128]{3,2,1,0:T(8,128)(2,1)S(1)}, u32[]{:S(2)}, u32[]{:S(2)}) collective-permute-start(bf16[1,1,528,128]{3,2,1,0:T(8,128)(2,1)S(1)} %maximum_bitcast_fusion), channel_id=1, source_target_pairs={{0,8},{8,16},{16,24},{24,32},{32,40},{40,48},{48,56},{56,64},{64,7... | collective-permute-start | bytes 405512 | tf_op jit(solution)/shard_map/ppermute | solution.py:18
  12.3 3.4 %convert_reduce_fusion = f32[2,64,128]{2,1,0:T(8,128)S(1)} fusion(bf16[2,64,128,128]{3,2,1,0:T(8,128)(2,1)} %param.6), kind=kLoop, calls=%fused_computation.20 | loop fusion | flops 4177920 | bytes 4259840 | tf_op jit(solution)/shard_map/reduce_sum | solution.py:117
  15.7 0.7 fusion.58
  16.4 0.6 convert_reduce_fusion.2
  18.2 19.8 %all-reduce.1 = (f32[]{:T(128)}, f32[]{:T(128)}) all-reduce(f32[]{:T(128)S(6)} %add.242, f32[]{:T(128)} %get-tuple-element.5), channel_id=1, replica_groups=mesh['gx'=32,'gy'=8] {'gy'}, use_global_device_ids=true, to_apply=%region_5.6 | all-reduce | flops 2 | bytes 16 | tf_op jit(solution)/shard_map/psum | solution.py:151
  38.0 68.3 %all-reduce = (f32[]{:T(128)}, f32[]{:T(128)}) all-reduce(f32[]{:T(128)} %get-tuple-element.9, f32[]{:T(128)} %get-tuple-element.10), channel_id=1, replica_groups=mesh['gx'=32,'gy'=8] {'gx'}, use_global_device_ids=true, to_apply=%region_6.7 | all-reduce | flops 2 | bytes 16 | tf_op jit(solution)/shard_map/psum | solution.py:151
  106.3 0.0 copy-done
  107.7 0.0 collective-permute-done.1
  107.7 0.0 collective-permute-done
  107.8 2.6 %collective-permute-start.3 = (bf16[3,1,528,128]{3,2,1,0:T(8,128)(2,1)S(1)}, bf16[3,1,528,128]{3,2,1,0:T(8,128)(2,1)S(1)}, u32[]{:S(2)}, u32[]{:S(2)}) collective-permute-start(bf16[3,1,528,128]{3,2,1,0:T(8,128)(2,1)S(1)} %pad_maximum_fusion.1), channel_id=1, source_target_pairs={{1,0},{2,1},{3,2},{4,3},{5,4},{6,5},{7,6},{9,8},{10,9},{11,10},{12... | collective-permute-start | bytes 1216520 | tf_op jit(solution)/shard_map/ppermute | solution.py:20
  110.3 3.3 %collective-permute-start.2 = (bf16[3,1,528,128]{3,2,1,0:T(8,128)(2,1)S(1)}, bf16[3,1,528,128]{3,2,1,0:T(8,128)(2,1)S(1)}, u32[]{:S(2)}, u32[]{:S(2)}) collective-permute-start(bf16[3,1,528,128]{3,2,1,0:T(8,128)(2,1)S(1)} %pad_maximum_fusion.1), channel_id=1, source_target_pairs={{0,1},{1,2},{2,3},{3,4},{4,5},{5,6},{6,7},{8,9},{9,10},{10,11},{11... | collective-permute-start | bytes 1216520 | tf_op jit(solution)/shard_map/ppermute | solution.py:18
  113.7 0.1 broadcast_multiply_fusion.3
  113.8 6.6 %collective-permute-done.3 = bf16[3,1,528,128]{3,2,1,0:T(8,128)(2,1)S(1)} collective-permute-done((bf16[3,1,528,128]{3,2,1,0:T(8,128)(2,1)S(1)}, bf16[3,1,528,128]{3,2,1,0:T(8,128)(2,1)S(1)}, u32[]{:S(2)}, u32[]{:S(2)}) %collective-permute-start.3) | collective-permute-done | bytes 405536 | tf_op jit(solution)/shard_map/ppermute | solution.py:20
  120.4 4.1 %collective-permute-done.2 = bf16[3,1,528,128]{3,2,1,0:T(8,128)(2,1)S(1)} collective-permute-done((bf16[3,1,528,128]{3,2,1,0:T(8,128)(2,1)S(1)}, bf16[3,1,528,128]{3,2,1,0:T(8,128)(2,1)S(1)}, u32[]{:S(2)}, u32[]{:S(2)}) %collective-permute-start.2) | collective-permute-done | bytes 405536 | tf_op jit(solution)/shard_map/ppermute | solution.py:18
  124.5 0.1 fusion.71
  124.6 0.1 fusion.54
  124.7 0.3 select_reduce_fusion
  125.0 0.1 pad_maximum_fusion
  125.2 0.8 multiply_convert_fusion
  126.0 1.1 multiply_reduce_fusion.1
  127.8 0.2 fusion.41
  128.0 0.2 fusion.47
  128.2 0.2 fusion.49
  128.4 0.2 fusion.40
  128.6 0.2 fusion.72
  128.8 0.2 fusion.73
  129.0 0.2 fusion.39
  129.2 0.2 fusion.74
  129.4 0.2 fusion.75
  129.6 0.2 fusion.38
  129.9 0.2 fusion.76
  130.1 0.2 fusion.77
  130.3 0.2 fusion.37
  130.5 0.2 fusion.78
  130.7 0.2 fusion.79
  131.0 0.2 fusion.36
  131.2 0.2 fusion.80
  131.4 0.3 convolution_bitcast_fusion.3
  131.6 0.2 convolution_bitcast_fusion.2
  131.8 0.2 fusion.44
  132.1 0.1 fusion.48
  132.2 1.3 collective-permute-start.5
  133.5 3.0 %collective-permute-start.4 = (bf16[1,1,128,128]{3,2,1,0:T(8,128)(2,1)S(1)}, bf16[1,1,128,128]{3,2,1,0:T(8,128)(2,1)S(1)}, u32[]{:S(2)}, u32[]{:S(2)}) collective-permute-start(bf16[1,1,128,128]{3,2,1,0:T(8,128)(2,1)S(1)} %fusion.48), channel_id=1, source_target_pairs={{0,8},{8,16},{16,24},{24,32},{32,40},{40,48},{48,56},{56,64},{64,7... | collective-permute-start | bytes 98312 | tf_op jit(solution)/shard_map/ppermute | solution.py:18
  136.5 17.4 %fusion.33 = (bf16[2,64,128,128]{3,2,1,0:T(8,128)(2,1)S(1)}, bf16[2,64,128,128]{3,2,1,0:T(8,128)(2,1)S(1)}, bf16[2,64,128,128]{3,2,1,0:T(8,128)(2,1)S(1)}, bf16[...) fusion(bf16[2,64,128,128]{3,2,1,0:T(8,128)(2,1)} %param.6, ...), kind=kLoop, calls=%fused_computation.36 | loop fusion | flops 41943040 | bytes 42303488 | tf_op jit(solution)/shard_map/convert_element_type | solution.py:127
  153.9 0.0 collective-permute-done.5
  153.9 0.0 collective-permute-done.4
  153.9 1.9 %collective-permute-start.6 = (bf16[3,1,128,128]{3,2,1,0:T(8,128)(2,1)S(1)}, bf16[3,1,128,128]{3,2,1,0:T(8,128)(2,1)S(1)}, u32[]{:S(2)}, u32[]{:S(2)}) collective-permute-start(bf16[3,1,128,128]{3,2,1,0:T(8,128)(2,1)S(1)} %pad_maximum_fusion.2), channel_id=1, source_target_pairs={{0,1},{1,2},{2,3},{3,4},{4,5},{5,6},{6,7},{8,9},{9,10},{10,11},{11... | collective-permute-start | bytes 294920 | tf_op jit(solution)/shard_map/ppermute | solution.py:18
  155.9 6.0 %collective-permute-start.7 = (bf16[3,1,128,128]{3,2,1,0:T(8,128)(2,1)S(1)}, bf16[3,1,128,128]{3,2,1,0:T(8,128)(2,1)S(1)}, u32[]{:S(2)}, u32[]{:S(2)}) collective-permute-start(bf16[3,1,128,128]{3,2,1,0:T(8,128)(2,1)S(1)} %pad_maximum_fusion.2), channel_id=1, source_target_pairs={{1,0},{2,1},{3,2},{4,3},{5,4},{6,5},{7,6},{9,8},{10,9},{11,10},{12... | collective-permute-start | bytes 294920 | tf_op jit(solution)/shard_map/ppermute | solution.py:20
  161.9 8.5 %fusion.6 = f32[2,64,128,128]{3,2,1,0:T(8,128)} fusion(bf16[384,128,1,1]{1,0,3,2:T(8,128)(2,1)S(1)} %bitcast.132, bf16[2,64,128,128]{3,2,1,0:T(8,128)(2,1)} %get-tuple-element.18, bf16[2,64,128,128]{3,2,1,0:T(8,128)(2,1)} %get-tuple-element.17, bf16[2,64,128,128]{3,2,1,0:T(8,128)(2,1)} %get-tuple-element.16), kind=kOutput, calls=%fused_computation.7 | convolution fusion | flops 1648361472 | bytes 21069824 | tf_op jit(solution)/shard_map/dot_general | solution.py:132
  170.4 0.0 collective-permute-done.6
  170.4 5.7 %fusion = f32[2,64,128,128]{3,2,1,0:T(8,128)} fusion(bf16[384,128,1,1]{1,0,3,2:T(8,128)(2,1)S(1)} %bitcast.140, bf16[2,64,128,128]{3,2,1,0:T(8,128)(2,1)S(1)} %get-tuple-element.15, bf16[2,64,128,128]{3,2,1,0:T(8,128)(2,1)S(1)} %get-tuple-element.14, bf16[2,64,128,128]{3,2,1,0:T(8,128)(2,1)S(1)} %get-tuple-element.21), kind=kOutput, calls=%fused_computation.1 | convolution fusion | flops 1648361472 | bytes 21069824 | tf_op jit(solution)/shard_map/dot_general | solution.py:132
  176.1 0.0 collective-permute-done.7
  176.1 11.4 %add_convert_fusion = bf16[2,64,128,128]{3,2,1,0:T(8,128)(2,1)} fusion(f32[2,64,128,128]{3,2,1,0:T(8,128)} %fusion.6, f32[2,64,128,128]{3,2,1,0:T(8,128)} %fusion, f32[2,64,128]{2,1,0:T(8,128)S(1)} %broadcast_multiply_fusion, bf16[384,128,1,1]{1,0,3,2:T(8,128)(2,1)S(1)} %bitcast.139, bf16[2,64,128,128]{3,2,1,0:T(8,128)(2,1)S(1)} %get-tuple-element.20, ...), kind=kOutput, calls=%fused_computation.39 | convolution fusion | flops 1656750080 | bytes 33718272 | tf_op jit(solution)/shard_map/dot_general | solution.py:132
  (19 shorter events, 0.2 us)
Async XLA Ops:
  0.0 106.3 %copy-start = (s32[64]{0:T(128)S(1)}, s32[64]{0:T(128)}, u32[]{:S(2)}) copy-start(s32[64]{0:T(128)} %param.11) | copy-start | bytes 772
  7.9 99.8 %collective-permute-start.1 = (bf16[1,1,528,128]{3,2,1,0:T(8,128)(2,1)S(1)}, bf16[1,1,528,128]{3,2,1,0:T(8,128)(2,1)S(1)}, u32[]{:S(2)}, u32[]{:S(2)}) collective-permute-start(bf16[1,1,528,128]{3,2,1,0:T(8,128)(2,1)S(1)} %maximum_bitcast_fusion), channel_id=1, source_target_pairs={{8,0},{16,8},{24,16},{32,24},{40,32},{48,40},{56,48},{64,56},{72,6... | collective-permute-start | bytes 405512 | tf_op jit(solution)/shard_map/ppermute | solution.py:20
  9.2 98.5 %collective-permute-start = (bf16[1,1,528,128]{3,2,1,0:T(8,128)(2,1)S(1)}, bf16[1,1,528,128]{3,2,1,0:T(8,128)(2,1)S(1)}, u32[]{:S(2)}, u32[]{:S(2)}) collective-permute-start(bf16[1,1,528,128]{3,2,1,0:T(8,128)(2,1)S(1)} %maximum_bitcast_fusion), channel_id=1, source_target_pairs={{0,8},{8,16},{16,24},{24,32},{32,40},{40,48},{48,56},{56,64},{64,7... | collective-permute-start | bytes 405512 | tf_op jit(solution)/shard_map/ppermute | solution.py:18
  107.8 12.6 %collective-permute-start.3 = (bf16[3,1,528,128]{3,2,1,0:T(8,128)(2,1)S(1)}, bf16[3,1,528,128]{3,2,1,0:T(8,128)(2,1)S(1)}, u32[]{:S(2)}, u32[]{:S(2)}) collective-permute-start(bf16[3,1,528,128]{3,2,1,0:T(8,128)(2,1)S(1)} %pad_maximum_fusion.1), channel_id=1, source_target_pairs={{1,0},{2,1},{3,2},{4,3},{5,4},{6,5},{7,6},{9,8},{10,9},{11,10},{12... | collective-permute-start | bytes 1216520 | tf_op jit(solution)/shard_map/ppermute | solution.py:20
  110.3 14.1 %collective-permute-start.2 = (bf16[3,1,528,128]{3,2,1,0:T(8,128)(2,1)S(1)}, bf16[3,1,528,128]{3,2,1,0:T(8,128)(2,1)S(1)}, u32[]{:S(2)}, u32[]{:S(2)}) collective-permute-start(bf16[3,1,528,128]{3,2,1,0:T(8,128)(2,1)S(1)} %pad_maximum_fusion.1), channel_id=1, source_target_pairs={{0,1},{1,2},{2,3},{3,4},{4,5},{5,6},{6,7},{8,9},{9,10},{10,11},{11... | collective-permute-start | bytes 1216520 | tf_op jit(solution)/shard_map/ppermute | solution.py:18
  132.2 21.7 %collective-permute-start.5 = (bf16[1,1,128,128]{3,2,1,0:T(8,128)(2,1)S(1)}, bf16[1,1,128,128]{3,2,1,0:T(8,128)(2,1)S(1)}, u32[]{:S(2)}, u32[]{:S(2)}) collective-permute-start(bf16[1,1,128,128]{3,2,1,0:T(8,128)(2,1)S(1)} %fusion.48), channel_id=1, source_target_pairs={{8,0},{16,8},{24,16},{32,24},{40,32},{48,40},{56,48},{64,56},{72,6... | collective-permute-start | bytes 98312 | tf_op jit(solution)/shard_map/ppermute | solution.py:20
  133.5 20.4 %collective-permute-start.4 = (bf16[1,1,128,128]{3,2,1,0:T(8,128)(2,1)S(1)}, bf16[1,1,128,128]{3,2,1,0:T(8,128)(2,1)S(1)}, u32[]{:S(2)}, u32[]{:S(2)}) collective-permute-start(bf16[1,1,128,128]{3,2,1,0:T(8,128)(2,1)S(1)} %fusion.48), channel_id=1, source_target_pairs={{0,8},{8,16},{16,24},{24,32},{32,40},{40,48},{48,56},{56,64},{64,7... | collective-permute-start | bytes 98312 | tf_op jit(solution)/shard_map/ppermute | solution.py:18
  153.9 16.5 %collective-permute-start.6 = (bf16[3,1,128,128]{3,2,1,0:T(8,128)(2,1)S(1)}, bf16[3,1,128,128]{3,2,1,0:T(8,128)(2,1)S(1)}, u32[]{:S(2)}, u32[]{:S(2)}) collective-permute-start(bf16[3,1,128,128]{3,2,1,0:T(8,128)(2,1)S(1)} %pad_maximum_fusion.2), channel_id=1, source_target_pairs={{0,1},{1,2},{2,3},{3,4},{4,5},{5,6},{6,7},{8,9},{9,10},{10,11},{11... | collective-permute-start | bytes 294920 | tf_op jit(solution)/shard_map/ppermute | solution.py:18
  155.9 20.2 %collective-permute-start.7 = (bf16[3,1,128,128]{3,2,1,0:T(8,128)(2,1)S(1)}, bf16[3,1,128,128]{3,2,1,0:T(8,128)(2,1)S(1)}, u32[]{:S(2)}, u32[]{:S(2)}) collective-permute-start(bf16[3,1,128,128]{3,2,1,0:T(8,128)(2,1)S(1)} %pad_maximum_fusion.2), channel_id=1, source_target_pairs={{1,0},{2,1},{3,2},{4,3},{5,4},{6,5},{7,6},{9,8},{10,9},{11,10},{12... | collective-permute-start | bytes 294920 | tf_op jit(solution)/shard_map/ppermute | solution.py:20
